TPU v7x, 128 devices: a whole 4x4x4 slice. The times are simulated.
128 devices in a mesh: belt: 16 (over x, z_lo, core), lon: 8 (over z_hi, y).
Axes of the slice: x: 4, y: 4, z: 4 (z_hi: 2, z_lo: 2; z = z_hi * 2 + z_lo), core: 2. Of those that a mesh axis runs over, the one named last changes fastest.
Arguments:
- grid_fields: bfloat16 [32, 2048, 4096], P(None, 'belt', 'lon'), may hold values from -6 to 6
- field_order: int32 [32], replicated, may hold values from 0 to 31, each once
- wave_order: int32 [1024], replicated, may hold values from 0 to 1023, as said below
Outputs:
- spectral: float32 [1024, 2, 32, 2, 512], P(('belt', 'lon'))
Inputs may be any that keep to these rules, and one draw needn't show every extreme that they name: wave_order is a permutation of the wavenumbers; each aligned block of 8 entries holds 4 wavenumbers m followed, in the same order, by their partners 1024 - 1 - m. field_order is a permutation.
All inputs are finite; a program needn't handle non-finite values.
Results may differ from a plain program's by a relative error of at most 0.0023.
Values may be sent and summed in bfloat16 or wider, within the bound.
A program may use at most 128 MiB of HBM per device.

v0:
```python
import math

import jax
import jax.numpy as jnp
from jax import lax
from jax.experimental import pallas as pl
from jax.experimental.pallas import tpu as pltpu
from jax.sharding import PartitionSpec as P

LANES = 128
NT_DIMS = (((1,), (1,)), ((), ()))

CODE_STEPS = 1024.0
CODE_LOW = -20.0

CHUNKS = 2
BLOCK = 32
RENORM = 16
EARLY = 19


def encode(value):
    magnitude = jnp.abs(value)
    exponent = jnp.floor(jnp.log(jnp.maximum(magnitude, 2.0**CODE_LOW)) * (1.0 / math.log(2.0)))
    exponent = jnp.maximum(exponent, CODE_LOW)
    code = jnp.round(((exponent - CODE_LOW) + magnitude * jnp.exp2(-exponent)) * CODE_STEPS)
    return jnp.where(value < 0.0, -code, code).astype(jnp.int32).astype(jnp.int16)


def decode(code):
    level = code.astype(jnp.int32).astype(jnp.float32) * (1.0 / CODE_STEPS)
    magnitude = jnp.abs(level)
    octave = jnp.maximum(jnp.floor(magnitude), 1.0)
    value = (magnitude - octave + 1.0) * jnp.exp2(octave + (CODE_LOW - 1.0))
    return jnp.where(level < 0.0, -value, value)


def split(value):
    high = value.astype(jnp.bfloat16)
    return high, (value - high.astype(jnp.float32)).astype(jnp.bfloat16)


def iota(shape, dim):
    return lax.broadcasted_iota(jnp.int32, shape, dim)


def column_of(waves, owner):
    return jnp.sum(jnp.where(iota(waves.shape, 1) == owner, waves, 0.0), axis=1, keepdims=True)


def fill_table(waves_ref, table_ref, slots, owners, lon_count):
    quarter = lon_count // 4
    coarse_count = quarter // LANES
    lane = iota((slots, LANES), 1)
    steps = (lane, lax.rem(lane, coarse_count) * LANES)

    def one_owner(owner):
        wave = jnp.broadcast_to(column_of(waves_ref[...], owner), (slots, LANES)).astype(jnp.int32)
        angles = [
            lax.rem(wave * step, lon_count).astype(jnp.float32) * (2.0 * math.pi / lon_count) for step in steps
        ]
        cos_fine, cos_coarse = [jnp.cos(angle) for angle in angles]
        sin_fine, sin_coarse = [jnp.sin(angle) for angle in angles]
        turn = lax.rem(wave, 4).astype(jnp.float32)
        turn = jnp.concatenate((turn, turn), axis=0)
        one = jnp.ones_like(turn)
        zero = jnp.zeros_like(turn)
        keep = jnp.where(turn == 0.0, one, jnp.where(turn == 2.0, -one, zero)).astype(jnp.bfloat16)
        swap = jnp.where(turn == 1.0, -one, jnp.where(turn == 3.0, one, zero)).astype(jnp.bfloat16)
        opposite = jnp.where((turn == 1.0) | (turn == 3.0), -one, one).astype(jnp.bfloat16)
        row = pl.multiple_of(owner * 2 * slots, 2 * slots)
        for a in range(coarse_count):
            ca = cos_coarse[:, a : a + 1]
            sa = sin_coarse[:, a : a + 1]
            cosine = ca * cos_fine - sa * sin_fine
            sine = sa * cos_fine + ca * sin_fine
            plain = jnp.concatenate((cosine, -sine), axis=0).astype(jnp.bfloat16)
            other = jnp.concatenate((sine, cosine), axis=0).astype(jnp.bfloat16)
            turned = plain * keep + other * swap
            for index, value in enumerate((plain, turned, plain * opposite, turned * opposite)):
                start = index * quarter + a * LANES
                table_ref[pl.ds(row, 2 * slots), start : start + LANES] = value

    @pl.loop(0, owners // 2)
    def _(pair):
        one_owner(2 * pair)
        one_owner(2 * pair + 1)


def start_legendre(wave, refs, mode_count, half):
    prev_ref, cur_ref, scale_ref, inv_ref, geo_ref, _ = refs
    lane = iota(wave.shape, 1).astype(jnp.float32)
    terms = None
    for a in range(mode_count // LANES):
        index = lane + (a * LANES + 1.0)
        term = jnp.where(index <= wave, jnp.log1p(0.5 / index), 0.0)
        terms = term if terms is None else terms + term
    start_sum = jnp.sum(terms, axis=1, keepdims=True)
    prev_ref[...] = jnp.zeros_like(prev_ref)
    cur_ref[...] = jnp.ones_like(cur_ref)
    inv_ref[...] = jnp.zeros_like(inv_ref)
    for a in range(half // LANES):
        lanes = slice(a * LANES, (a + 1) * LANES)
        colatitude = (math.pi / (2 * half + 0.5)) * (lane + (a * LANES + 0.75))
        sine = jnp.sin(colatitude)
        geo_ref[0, :, lanes] = jnp.cos(colatitude)
        geo_ref[1, :, lanes] = (math.pi / (2 * half + 0.5) * math.sqrt(half)) * sine
        scale_ref[:, lanes] = -0.5 * math.log(2.0) + 0.5 * start_sum + wave * jnp.log(sine)


def legendre_block(step, wave, refs, table_ref, mode_count, half):
    prev_ref, cur_ref, scale_ref, inv_ref, geo_ref, rows_ref = refs
    slots = wave.shape[0]
    first = (step * BLOCK).astype(jnp.float32)
    chunks = half // LANES
    lanes = [slice(a * LANES, (a + 1) * LANES) for a in range(chunks)]
    inverse = inv_ref[...]
    prev = [prev_ref[:, s] for s in lanes]
    cur = [cur_ref[:, s] for s in lanes]
    amp = [None] * chunks
    for row in range(BLOCK):
        if row % RENORM == 0:
            for a in range(chunks):
                total = jnp.maximum(jnp.abs(prev[a]) + jnp.abs(cur[a]), 1e-30)
                prev[a] = prev[a] / total
                cur[a] = cur[a] / total
                log_scale = scale_ref[:, lanes[a]] + jnp.log(total)
                scale_ref[:, lanes[a]] = log_scale
                amp[a] = jnp.exp(log_scale) * geo_ref[1, :, lanes[a]]
        for a in range(chunks):
            rows_ref[a, row * slots : (row + 1) * slots, :] = cur[a] * amp[a]
        offset = first + (row + 1.0)
        degree = wave + offset
        numer = 4.0 * degree * degree - 1.0
        denom = offset * (wave + degree)
        root = lax.rsqrt(numer * denom)
        factor = jnp.where(degree < mode_count, numer * root, 0.0)
        ratio = factor * inverse
        inverse = denom * root
        for a in range(chunks):
            following = (factor * geo_ref[0, :, lanes[a]]) * cur[a] - ratio * prev[a]
            prev[a] = cur[a]
            cur[a] = following
    inv_ref[...] = inverse
    for a in range(chunks):
        prev_ref[:, lanes[a]] = prev[a]
        cur_ref[:, lanes[a]] = cur[a]
    out_row = pl.multiple_of(step * (BLOCK // 2), BLOCK // 2)
    for slot in range(slots):
        for parity in range(2):
            for a in range(chunks):
                table_ref[slot, parity, pl.ds(out_row, BLOCK // 2), lanes[a]] = rows_ref[
                    a, pl.ds(parity * slots + slot, BLOCK // 2, stride=2 * slots), :
                ].astype(jnp.bfloat16)


def analyse(grid_fields, waves, order_lanes):
    belts = lax.axis_size("belt")
    lons = lax.axis_size("lon")
    levels, lat_local, lon_local = grid_fields.shape
    owners = belts * lons
    slots = waves.shape[0]
    lat_count = lat_local * belts
    half = lat_count // 2
    lon_count = lon_local * lons
    mode_count = slots * owners
    half_modes = mode_count // 2
    items = levels // lons
    chunk_items = items // CHUNKS
    chunk_rows = chunk_items * lat_local
    group = 2 * lons
    blocks = owners // group
    owner_rows = 2 * slots
    block_rows = group * owner_rows
    rows = 2 * levels
    half_lons = lons // 2
    piece = lat_local // 2
    scale = 1.0 / math.sqrt(lon_count)
    mesh_id = pl.DeviceIdType.MESH
    legendre_steps = mode_count // BLOCK

    def body(
        fields_ref, waves_ref, order_ref, out_ref, dft_ref, leg_ref, rows_in_ref, send_ref, recv_ref, wide_ref,
        prev_ref, cur_ref, scale_ref, inv_ref, geo_ref, step_rows_ref,
        in_send, in_recv, in_local, out_send, out_recv, out_local,
    ):
        belt = lax.axis_index("belt")
        lon = lax.axis_index("lon")
        me = belt * lons + lon
        barrier = pltpu.get_barrier_semaphore()
        refs = (prev_ref, cur_ref, scale_ref, inv_ref, geo_ref, step_rows_ref)

        def lon_away(away):
            high = lax.rem(lon // half_lons + away // half_lons, 2)
            return high * half_lons + lax.rem(lax.rem(lon, half_lons) + lax.rem(away, half_lons), half_lons)

        def place(step):
            away = blocks - 1 - step
            x = lax.rem(belt // 4 + away // 2, blocks // 2)
            return x * 2 + lax.rem(lax.rem(belt // 2, 2) + lax.rem(away, 2), 2)

        def member(index):
            return lax.rem(lax.rem(belt, 2) + index // lons, 2), lon_away(lax.rem(index, lons))

        def gather(chunk, away, item, part):
            target = lon_away(away)
            return pltpu.make_async_remote_copy(
                fields_ref.at[target * items + chunk * chunk_items + item, pl.ds(part * piece, piece)],
                rows_in_ref.at[chunk, lon, pl.ds(item * lat_local + part * piece, piece)],
                in_send.at[chunk],
                in_recv.at[chunk],
                device_id=(belt, target),
                device_id_type=mesh_id,
            )

        def own_rows(chunk, item):
            return pltpu.make_async_copy(
                fields_ref.at[lon * items + chunk * chunk_items + item],
                rows_in_ref.at[chunk, lon, pl.ds(item * lat_local, lat_local)],
                in_local.at[chunk, item],
            )

        def send(chunk, step, index):
            core, target = member(index)
            return pltpu.make_async_remote_copy(
                send_ref.at[chunk, step, core * lons + target],
                recv_ref.at[chunk, me],
                out_send.at[chunk],
                out_recv.at[chunk],
                device_id=(place(step) * 2 + core, target),
                device_id_type=mesh_id,
            )

        def own_block(chunk):
            core, target = member(0)
            return pltpu.make_async_copy(
                send_ref.at[chunk, blocks - 1, core * lons + target], recv_ref.at[chunk, me], out_local.at[chunk]
            )

        def gathered(chunk):
            whole = rows_in_ref.at[chunk, pl.ds(0, lons - 1)]
            return pltpu.make_async_remote_copy(
                whole, whole, in_send.at[chunk], in_recv.at[chunk],
                device_id=(belt, lon_away(1)), device_id_type=mesh_id,
            )

        def exchanged(chunk):
            whole = recv_ref.at[chunk, pl.ds(0, owners - 1)]
            return pltpu.make_async_remote_copy(
                whole, whole, out_send.at[chunk], out_recv.at[chunk],
                device_id=(belt, lon_away(1)), device_id_type=mesh_id,
            )

        def legendre_range(start, stop):
            wave = jnp.broadcast_to(column_of(waves_ref[...], me), (slots, LANES))

            @pl.loop(start, stop)
            def _(step):
                legendre_block(step, wave, refs, leg_ref, mode_count, half)

        def transform(chunk):
            for item in range(chunk_items):
                own_rows(chunk, item).wait()
            gathered(chunk).wait_recv()

            @pl.loop(0, blocks)
            def _(step):
                start = pl.multiple_of(place(step) * block_rows, block_rows)
                total = None
                for part in range(lons):
                    term = lax.dot_general(
                        dft_ref[pl.ds(start, block_rows), part * lon_local : (part + 1) * lon_local],
                        rows_in_ref[chunk, part],
                        NT_DIMS,
                        preferred_element_type=jnp.float32,
                    )
                    total = term if total is None else total + term
                send_ref[chunk, step] = encode(total * scale).reshape(group, owner_rows, chunk_rows)

                @pl.loop(0, group)
                def _(back):
                    index = group - 1 - back

                    @pl.when((step < blocks - 1) | (index > 0))
                    def _():
                        send(chunk, step, index).start()

            own_block(chunk).start()

        def mirror_sums(chunk):
            own_block(chunk).wait()
            exchanged(chunk).wait_recv()
            mirror = (iota((lat_local, lat_local), 0) + iota((lat_local, lat_local), 1)).astype(jnp.float32)
            mirror = jnp.where(mirror == lat_local - 1.0, 1.0, 0.0).astype(jnp.bfloat16)

            @pl.loop(0, belts // 2)
            def _(near):
                far = belts - 1 - near
                for item in range(chunk_items):
                    lanes = slice(item * lat_local, (item + 1) * lat_local)
                    north = decode(recv_ref[chunk, pl.ds(near * lons, lons), :, lanes]).reshape(-1, lat_local)
                    south = decode(recv_ref[chunk, pl.ds(far * lons, lons), :, lanes]).reshape(-1, lat_local)
                    high, low = split(south)
                    south = jnp.dot(high, mirror, preferred_element_type=jnp.float32) + jnp.dot(
                        low, mirror, preferred_element_type=jnp.float32
                    )
                    wide_ref[0, near, chunk * chunk_items + item] = north + south
                    wide_ref[1, near, chunk * chunk_items + item] = north - south

        @pl.loop(1, owners)
        def _(away):
            peer = lax.rem(me + away, owners)
            pl.semaphore_signal(
                barrier, inc=1, device_id=(peer // lons, lax.rem(peer, lons)), device_id_type=mesh_id
            )

        for chunk in range(CHUNKS):
            for item in range(chunk_items):
                own_rows(chunk, item).start()
        start_legendre(
            jnp.broadcast_to(column_of(waves_ref[...], me), (slots, LANES)), refs, mode_count, half
        )
        pl.semaphore_wait(barrier, owners - 1)

        @pl.loop(0, CHUNKS * chunk_items * 2)
        def _(index):
            chunk = index // (2 * chunk_items)
            item = lax.rem(index // 2, chunk_items)

            @pl.loop(1, lons)
            def _(away):
                gather(chunk, lons - away, item, lax.rem(index, 2)).start()

        fill_table(waves_ref, dft_ref, slots, owners, lon_count)
        legendre_range(0, EARLY)
        transform(0)
        legendre_range(EARLY, legendre_steps)
        transform(1)
        mirror_sums(0)
        mirror_sums(1)

        source = iota((2 * rows, 2 * rows), 0)
        target = iota((2 * rows, 2 * rows), 1)
        within = lax.rem(source, rows)
        level = lax.rem(within // 2, lons) * items + within // (2 * lons)
        match = (
            (level == order_ref[...])
            & (lax.rem(within, 2) == lax.rem(target, rows) // levels)
            & (source // rows == target // rows)
        )
        order = jnp.where(match, 1.0, 0.0).T.astype(jnp.bfloat16)

        @pl.loop(0, slots)
        def _(slot):
            for parity in range(2):
                value = jnp.concatenate(
                    [
                        jnp.concatenate(
                            [
                                wide_ref[parity, near, item, pl.ds(slot, 2 * lons, stride=slots), :]
                                for item in range(items)
                            ],
                            axis=0,
                        )
                        for near in range(belts // 2)
                    ],
                    axis=1,
                )
                sums = jnp.dot(
                    order, jnp.concatenate(split(value), axis=0), preferred_element_type=jnp.float32
                ).astype(jnp.bfloat16)
                result = lax.dot_general(sums, leg_ref[slot, parity], NT_DIMS, preferred_element_type=jnp.float32)
                out_ref[slot, :, parity * half_modes : (parity + 1) * half_modes] = result[:rows] + result[rows:]

        for chunk in range(CHUNKS):
            gathered(chunk).wait_send()
            exchanged(chunk).wait_send()

    dma = pltpu.SemaphoreType.DMA
    return pl.pallas_call(
        body,
        name="analyse",
        in_specs=[
            pl.BlockSpec(memory_space=pl.ANY),
            pl.BlockSpec(memory_space=pltpu.VMEM),
            pl.BlockSpec(memory_space=pltpu.VMEM),
        ],
        out_specs=pl.BlockSpec(memory_space=pltpu.VMEM),
        out_shape=jax.ShapeDtypeStruct((slots, rows, mode_count), jnp.float32),
        scratch_shapes=[
            pltpu.VMEM((owners * owner_rows, lon_count), jnp.bfloat16),
            pltpu.VMEM((slots, 2, half_modes, half), jnp.bfloat16),
            pltpu.VMEM((CHUNKS, lons, chunk_rows, lon_local), jnp.bfloat16),
            pltpu.VMEM((CHUNKS, blocks, group, owner_rows, chunk_rows), jnp.int16),
            pltpu.VMEM((CHUNKS, owners, owner_rows, chunk_rows), jnp.int16),
            pltpu.VMEM((2, belts // 2, items, 2 * lons * slots, lat_local), jnp.float32),
            pltpu.VMEM((slots, half), jnp.float32),
            pltpu.VMEM((slots, half), jnp.float32),
            pltpu.VMEM((slots, half), jnp.float32),
            pltpu.VMEM((slots, LANES), jnp.float32),
            pltpu.VMEM((2, slots, half), jnp.float32),
            pltpu.VMEM((half // LANES, BLOCK * slots, LANES), jnp.float32),
            dma((CHUNKS,)),
            dma((CHUNKS,)),
            dma((CHUNKS, chunk_items)),
            dma((CHUNKS,)),
            dma((CHUNKS,)),
            dma((CHUNKS,)),
        ],
        compiler_params=pltpu.CompilerParams(
            collective_id=0, has_side_effects=True, vmem_limit_bytes=60 << 20
        ),
    )(grid_fields, waves, order_lanes)


def on_device(grid_fields, field_order, wave_order):
    owners = lax.axis_size("belt") * lax.axis_size("lon")
    mode_count = wave_order.shape[0]
    slots = mode_count // owners
    levels = grid_fields.shape[0]
    waves = wave_order.astype(jnp.float32).reshape(owners, slots).T
    spectral = analyse(grid_fields, waves, jnp.tile(field_order.astype(jnp.int32), 4)[None, :])
    return spectral.reshape(slots, 2, levels, 2, mode_count // 2)


def solution(mesh):
    return jax.shard_map(
        on_device,
        mesh=mesh,
        in_specs=(P(None, "belt", "lon"), P(), P()),
        out_specs=P(("belt", "lon"), None, None, None, None),
        check_vma=False,
    )
```

profile of v0, /device:TPU:1, one launch (start us, length us, event | category | flops | bytes accessed | tf_op | source)
XLA Modules:
  0.0 104.7 jit_solution(5958920918645363659)
XLA Ops:
  0.0 0.7 tile.2
  0.7 0.6 broadcast_in_dim_tile.3.order_ref
  1.3 0.7 convert_element_type.3
  1.9 0.1 reshape.7
  2.0 0.7 copy.4
  2.7 98.0 %analyse.1 = f32[8,64,1024]{2,1,0:T(8,128)} custom-call(bf16[32,128,512]{2,1,0:T(8,128)(2,1)} %fields_ref.1, f32[8,128]{1,0:T(8,128)} %bitcast.1, s32[1,128]{1,0:T(1,128)} %broadcast_in_dim_tile.3.order_ref), custom_call_target="tpu_custom_call" | custom-call | tf_op jit(solution)/shard_map/analyse/pallas_call | solution.py:380
  100.7 4.0 %reshape.8 = f32[8,2,32,2,512]{4,3,2,1,0:T(2,128)} reshape(f32[8,64,1024]{2,1,0:T(8,128)} %analyse.1) | data formatting | bytes 4194304 | tf_op jit(solution)/shard_map/reshape | solution.py:423
where the time goes:
time: 105 us
  Pallas kernels  98 us (93%)
  local copies, waits for them, and re-layouts  5.99 us (6%)
    pallas_call x1, Pallas kernels, analyse(): pl.pallas_call(body, name='analyse', in_specs=[pl.BlockSpec(memory_space=...  98 us
    reshape x1, local copies, waits for them, and re-layouts, on_device(): return spectral.reshape(slots, 2, levels, 2, mode_count // 2)  3.99 us

commit v1 on v0

--- a/solution.py
+++ b/solution.py
@@ -44,8 +44,13 @@
     return lax.broadcasted_iota(jnp.int32, shape, dim)
 
 
-def column_of(waves, owner):
-    return jnp.sum(jnp.where(iota(waves.shape, 1) == owner, waves, 0.0), axis=1, keepdims=True)
+def column_of(waves, owner, slots):
+    waves = waves.astype(jnp.float32)
+    per_row = LANES // slots
+    row = jnp.sum(jnp.where(iota(waves.shape, 0) == owner // per_row, waves, 0.0), axis=0, keepdims=True)
+    shape = (slots, LANES)
+    mine = iota(shape, 1) == lax.rem(owner, per_row) * slots + iota(shape, 0)
+    return jnp.sum(jnp.where(mine, jnp.broadcast_to(row, shape), 0.0), axis=1, keepdims=True)
 
 
 def fill_table(waves_ref, table_ref, slots, owners, lon_count):
@@ -55,7 +60,7 @@
     steps = (lane, lax.rem(lane, coarse_count) * LANES)
 
     def one_owner(owner):
-        wave = jnp.broadcast_to(column_of(waves_ref[...], owner), (slots, LANES)).astype(jnp.int32)
+        wave = jnp.broadcast_to(column_of(waves_ref[...], owner, slots), (slots, LANES)).astype(jnp.int32)
         angles = [
             lax.rem(wave * step, lon_count).astype(jnp.float32) * (2.0 * math.pi / lon_count) for step in steps
         ]
@@ -154,16 +159,16 @@
                 ].astype(jnp.bfloat16)
 
 
-def analyse(grid_fields, waves, order_lanes):
+def analyse(grid_fields, waves, field_order):
     belts = lax.axis_size("belt")
     lons = lax.axis_size("lon")
     levels, lat_local, lon_local = grid_fields.shape
     owners = belts * lons
-    slots = waves.shape[0]
+    mode_count = waves.shape[0] * waves.shape[1]
+    slots = mode_count // owners
     lat_count = lat_local * belts
     half = lat_count // 2
     lon_count = lon_local * lons
-    mode_count = slots * owners
     half_modes = mode_count // 2
     items = levels // lons
     chunk_items = items // CHUNKS
@@ -174,15 +179,16 @@
     block_rows = group * owner_rows
     rows = 2 * levels
     half_lons = lons // 2
+    side_belts = belts // 4
     piece = lat_local // 2
     scale = 1.0 / math.sqrt(lon_count)
     mesh_id = pl.DeviceIdType.MESH
     legendre_steps = mode_count // BLOCK
 
     def body(
-        fields_ref, waves_ref, order_ref, out_ref, dft_ref, leg_ref, rows_in_ref, send_ref, recv_ref, wide_ref,
+        fields_ref, waves_ref, order_ref, out_ref, dft_ref, leg_ref, rows_in_ref, send_ref, recv_ref, wide_ref, sum_ref,
         prev_ref, cur_ref, scale_ref, inv_ref, geo_ref, step_rows_ref,
-        in_send, in_recv, in_local, out_send, out_recv, out_local,
+        in_send, in_recv, in_local, out_send, out_recv, out_local, ready,
     ):
         belt = lax.axis_index("belt")
         lon = lax.axis_index("lon")
@@ -194,10 +200,13 @@
             high = lax.rem(lon // half_lons + away // half_lons, 2)
             return high * half_lons + lax.rem(lax.rem(lon, half_lons) + lax.rem(away, half_lons), half_lons)
 
+        side = lax.rem((belt // 4 + 1) // 2, 2)
+
         def place(step):
-            away = blocks - 1 - step
-            x = lax.rem(belt // 4 + away // 2, blocks // 2)
-            return x * 2 + lax.rem(lax.rem(belt // 2, 2) + lax.rem(away, 2), 2)
+            turn = step // 2
+            high = lax.rem(belt // 8 + lax.rem(turn + 1, 2), 2)
+            low = lax.rem(lax.rem(belt // 4, 2) + lax.rem((turn + 1) // 2, 2), 2)
+            return high * 4 + low * 2 + lax.rem(lax.rem(belt // 2, 2) + lax.rem(step + 1, 2), 2)
 
         def member(index):
             return lax.rem(lax.rem(belt, 2) + index // lons, 2), lon_away(lax.rem(index, lons))
@@ -226,7 +235,7 @@
                 send_ref.at[chunk, step, core * lons + target],
                 recv_ref.at[chunk, me],
                 out_send.at[chunk],
-                out_recv.at[chunk],
+                out_recv.at[chunk, side],
                 device_id=(place(step) * 2 + core, target),
                 device_id_type=mesh_id,
             )
@@ -244,15 +253,15 @@
                 device_id=(belt, lon_away(1)), device_id_type=mesh_id,
             )
 
-        def exchanged(chunk):
-            whole = recv_ref.at[chunk, pl.ds(0, owners - 1)]
+        def exchanged(chunk, from_side, count):
+            whole = recv_ref.at[chunk, pl.ds(0, count)]
             return pltpu.make_async_remote_copy(
-                whole, whole, out_send.at[chunk], out_recv.at[chunk],
+                whole, whole, out_send.at[chunk], out_recv.at[chunk, from_side],
                 device_id=(belt, lon_away(1)), device_id_type=mesh_id,
             )
 
         def legendre_range(start, stop):
-            wave = jnp.broadcast_to(column_of(waves_ref[...], me), (slots, LANES))
+            wave = jnp.broadcast_to(column_of(waves_ref[...], me, slots), (slots, LANES))
 
             @pl.loop(start, stop)
             def _(step):
@@ -287,14 +296,13 @@
 
             own_block(chunk).start()
 
-        def mirror_sums(chunk):
-            own_block(chunk).wait()
-            exchanged(chunk).wait_recv()
+        def mirror_sums(chunk, from_side):
             mirror = (iota((lat_local, lat_local), 0) + iota((lat_local, lat_local), 1)).astype(jnp.float32)
             mirror = jnp.where(mirror == lat_local - 1.0, 1.0, 0.0).astype(jnp.bfloat16)
 
-            @pl.loop(0, belts // 2)
-            def _(near):
+            @pl.loop(0, side_belts)
+            def _(index):
+                near = from_side * side_belts + index
                 far = belts - 1 - near
                 for item in range(chunk_items):
                     lanes = slice(item * lat_local, (item + 1) * lat_local)
@@ -307,20 +315,58 @@
                     wide_ref[0, near, chunk * chunk_items + item] = north + south
                     wide_ref[1, near, chunk * chunk_items + item] = north - south
 
-        @pl.loop(1, owners)
+        def project(from_side, order, emit):
+            start = pl.multiple_of(from_side * side_belts * lat_local, LANES)
+
+            @pl.loop(0, slots)
+            def _(slot):
+                for parity in range(2):
+                    value = jnp.concatenate(
+                        [
+                            jnp.concatenate(
+                                [
+                                    wide_ref[
+                                        parity, from_side * side_belts + near, item,
+                                        pl.ds(slot, 2 * lons, stride=slots), :,
+                                    ]
+                                    for item in range(items)
+                                ],
+                                axis=0,
+                            )
+                            for near in range(side_belts)
+                        ],
+                        axis=1,
+                    )
+                    sums = jnp.dot(
+                        order, jnp.concatenate(split(value), axis=0), preferred_element_type=jnp.float32
+                    ).astype(jnp.bfloat16)
+                    result = lax.dot_general(
+                        sums,
+                        leg_ref[slot, parity, :, pl.ds(start, side_belts * lat_local)],
+                        NT_DIMS,
+                        preferred_element_type=jnp.float32,
+                    )
+                    emit(slot, parity, result[:rows] + result[rows:])
+
+        def belt_peers(semaphore):
+            @pl.loop(1, belts)
+            def _(away):
+                peer = (lax.rem(belt + away, belts), lon)
+                pl.semaphore_signal(semaphore, inc=1, device_id=peer, device_id_type=mesh_id)
+
+        @pl.loop(1, lons)
         def _(away):
-            peer = lax.rem(me + away, owners)
-            pl.semaphore_signal(
-                barrier, inc=1, device_id=(peer // lons, lax.rem(peer, lons)), device_id_type=mesh_id
-            )
+            pl.semaphore_signal(barrier, inc=1, device_id=(belt, lon_away(away)), device_id_type=mesh_id)
+
+        belt_peers(barrier)
 
         for chunk in range(CHUNKS):
             for item in range(chunk_items):
                 own_rows(chunk, item).start()
         start_legendre(
-            jnp.broadcast_to(column_of(waves_ref[...], me), (slots, LANES)), refs, mode_count, half
+            jnp.broadcast_to(column_of(waves_ref[...], me, slots), (slots, LANES)), refs, mode_count, half
         )
-        pl.semaphore_wait(barrier, owners - 1)
+        pl.semaphore_wait(barrier, lons + belts - 2)
 
         @pl.loop(0, CHUNKS * chunk_items * 2)
         def _(index):
@@ -331,50 +377,52 @@
             def _(away):
                 gather(chunk, lons - away, item, lax.rem(index, 2)).start()
 
+        belt_peers(ready)
         fill_table(waves_ref, dft_ref, slots, owners, lon_count)
         legendre_range(0, EARLY)
+        pl.semaphore_wait(ready, belts - 1)
         transform(0)
         legendre_range(EARLY, legendre_steps)
         transform(1)
-        mirror_sums(0)
-        mirror_sums(1)
 
         source = iota((2 * rows, 2 * rows), 0)
         target = iota((2 * rows, 2 * rows), 1)
+        wanted = jnp.zeros((1, 2 * rows), jnp.int32)
+        for index in range(levels):
+            wanted = jnp.where(lax.rem(iota((1, 2 * rows), 1), levels) == index, order_ref[index], wanted)
         within = lax.rem(source, rows)
         level = lax.rem(within // 2, lons) * items + within // (2 * lons)
         match = (
-            (level == order_ref[...])
+            (level == wanted)
             & (lax.rem(within, 2) == lax.rem(target, rows) // levels)
             & (source // rows == target // rows)
         )
         order = jnp.where(match, 1.0, 0.0).T.astype(jnp.bfloat16)
 
-        @pl.loop(0, slots)
-        def _(slot):
-            for parity in range(2):
-                value = jnp.concatenate(
-                    [
-                        jnp.concatenate(
-                            [
-                                wide_ref[parity, near, item, pl.ds(slot, 2 * lons, stride=slots), :]
-                                for item in range(items)
-                            ],
-                            axis=0,
-                        )
-                        for near in range(belts // 2)
-                    ],
-                    axis=1,
-                )
-                sums = jnp.dot(
-                    order, jnp.concatenate(split(value), axis=0), preferred_element_type=jnp.float32
-                ).astype(jnp.bfloat16)
-                result = lax.dot_general(sums, leg_ref[slot, parity], NT_DIMS, preferred_element_type=jnp.float32)
-                out_ref[slot, :, parity * half_modes : (parity + 1) * half_modes] = result[:rows] + result[rows:]
+        other_count = owners // 2
+        for chunk in range(CHUNKS):
+            exchanged(chunk, 1 - side, other_count).wait_recv()
+            mirror_sums(chunk, 1 - side)
+            if chunk < CHUNKS - 1:
+                own_block(chunk).wait()
+                exchanged(chunk, side, other_count - 1).wait_recv()
+                mirror_sums(chunk, side)
+
+        def keep(slot, parity, value):
+            sum_ref[slot, parity] = value
+
+        def finish(slot, parity, value):
+            out_ref[slot, :, parity, :] = sum_ref[slot, parity] + value
+
+        project(1 - side, order, keep)
+        own_block(CHUNKS - 1).wait()
+        exchanged(CHUNKS - 1, side, other_count - 1).wait_recv()
+        mirror_sums(CHUNKS - 1, side)
+        project(side, order, finish)
 
         for chunk in range(CHUNKS):
             gathered(chunk).wait_send()
-            exchanged(chunk).wait_send()
+            exchanged(chunk, side, owners - 1).wait_send()
 
     dma = pltpu.SemaphoreType.DMA
     return pl.pallas_call(
@@ -383,10 +431,10 @@
         in_specs=[
             pl.BlockSpec(memory_space=pl.ANY),
             pl.BlockSpec(memory_space=pltpu.VMEM),
-            pl.BlockSpec(memory_space=pltpu.VMEM),
+            pl.BlockSpec(memory_space=pltpu.SMEM),
         ],
         out_specs=pl.BlockSpec(memory_space=pltpu.VMEM),
-        out_shape=jax.ShapeDtypeStruct((slots, rows, mode_count), jnp.float32),
+        out_shape=jax.ShapeDtypeStruct((slots, rows, 2, half_modes), jnp.float32),
         scratch_shapes=[
             pltpu.VMEM((owners * owner_rows, lon_count), jnp.bfloat16),
             pltpu.VMEM((slots, 2, half_modes, half), jnp.bfloat16),
@@ -394,6 +442,7 @@
             pltpu.VMEM((CHUNKS, blocks, group, owner_rows, chunk_rows), jnp.int16),
             pltpu.VMEM((CHUNKS, owners, owner_rows, chunk_rows), jnp.int16),
             pltpu.VMEM((2, belts // 2, items, 2 * lons * slots, lat_local), jnp.float32),
+            pltpu.VMEM((slots, 2, rows, half_modes), jnp.float32),
             pltpu.VMEM((slots, half), jnp.float32),
             pltpu.VMEM((slots, half), jnp.float32),
             pltpu.VMEM((slots, half), jnp.float32),
@@ -404,13 +453,14 @@
             dma((CHUNKS,)),
             dma((CHUNKS, chunk_items)),
             dma((CHUNKS,)),
+            dma((CHUNKS, 2)),
             dma((CHUNKS,)),
-            dma((CHUNKS,)),
+            pltpu.SemaphoreType.REGULAR,
         ],
         compiler_params=pltpu.CompilerParams(
             collective_id=0, has_side_effects=True, vmem_limit_bytes=60 << 20
         ),
-    )(grid_fields, waves, order_lanes)
+    )(grid_fields, waves, field_order)
 
 
 def on_device(grid_fields, field_order, wave_order):
@@ -418,8 +468,8 @@
     mode_count = wave_order.shape[0]
     slots = mode_count // owners
     levels = grid_fields.shape[0]
-    waves = wave_order.astype(jnp.float32).reshape(owners, slots).T
-    spectral = analyse(grid_fields, waves, jnp.tile(field_order.astype(jnp.int32), 4)[None, :])
+    waves = wave_order.astype(jnp.int32).reshape(mode_count // LANES, LANES)
+    spectral = analyse(grid_fields, waves, field_order.astype(jnp.int32))
     return spectral.reshape(slots, 2, levels, 2, mode_count // 2)
 
 

time: 105 us -> 98.4 us (0.937)
  Pallas kernels: 98 us -> 94.4 us
  local copies, waits for them, and re-layouts: 5.99 us -> 3.81 us
    reshape x3 -> x0, local copies, waits for them, and re-layouts: 4.73 us -> none  [the longest x1 3.99 us: on_device(): return spectral.reshape(slots, 2, levels, 2, mode_count // 2)]
    unnamed x0 -> x1, local copies, waits for them, and re-layouts: none -> 3.81 us
    pallas_call x1, Pallas kernels: 98 us -> 94.4 us  [analyse(): pl.pallas_call(body, name='analyse', in_specs=[pl.BlockSpec(memory_space=...]
    another operation x2 -> x0, local copies, waits for them, and re-layouts: 1.26 us -> none  [on_device(): jnp.tile(field_order.astype(jnp.int32), 4)[None, :]]
where the time goes in v1:
time: 98.4 us; the launch traced here: 98.2 us
  Pallas kernels  94.4 us (96%)
  local copies, waits for them, and re-layouts  3.81 us (4%)
    pallas_call x1, Pallas kernels, analyse(): pl.pallas_call(body, name='analyse', in_specs=[pl.BlockSpec(memory_space=...  94.4 us
    unnamed x1, local copies, waits for them, and re-layouts  3.81 us

profile of v1, /device:TPU:1, one launch (start us, length us, event | category | flops | bytes accessed | tf_op | source)
XLA Modules:
  0.0 98.2 jit_solution(17080778654076028857)
XLA Ops:
  0.0 94.4 %analyse.1 = f32[8,64,2,512]{3,2,1,0:T(2,128)} custom-call(bf16[32,128,512]{2,1,0:T(8,128)(2,1)} %fields_ref.1, s32[8,128]{1,0:T(8,128)} %bitcast.3, s32[32]{0:T(128)} %order_ref.1), custom_call_target="tpu_custom_call" | custom-call | tf_op jit(solution)/shard_map/analyse/pallas_call | solution.py:428
  94.4 3.8 %copy.5 = f32[8,2,32,2,512]{4,3,2,1,0:T(2,128)} copy(f32[8,2,32,2,512]{4,3,2,1,0:T(2,128)} %bitcast.2) | data formatting | bytes 4194304

commit v2 on v1

--- a/solution.py
+++ b/solution.py
@@ -186,9 +186,9 @@
     legendre_steps = mode_count // BLOCK
 
     def body(
-        fields_ref, waves_ref, order_ref, out_ref, dft_ref, leg_ref, rows_in_ref, send_ref, recv_ref, wide_ref, sum_ref,
+        fields_ref, waves_in_ref, order_in_ref, out_ref, waves_ref, order_ref, dft_ref, leg_ref, rows_in_ref, send_ref, recv_ref, wide_ref, sum_ref,
         prev_ref, cur_ref, scale_ref, inv_ref, geo_ref, step_rows_ref,
-        in_send, in_recv, in_local, out_send, out_recv, out_local, ready,
+        in_send, in_recv, in_local, out_send, out_recv, out_local, small, ready,
     ):
         belt = lax.axis_index("belt")
         lon = lax.axis_index("lon")
@@ -300,7 +300,7 @@
             mirror = (iota((lat_local, lat_local), 0) + iota((lat_local, lat_local), 1)).astype(jnp.float32)
             mirror = jnp.where(mirror == lat_local - 1.0, 1.0, 0.0).astype(jnp.bfloat16)
 
-            @pl.loop(0, side_belts)
+            @pl.loop(0, side_belts, unroll=4)
             def _(index):
                 near = from_side * side_belts + index
                 far = belts - 1 - near
@@ -318,7 +318,7 @@
         def project(from_side, order, emit):
             start = pl.multiple_of(from_side * side_belts * lat_local, LANES)
 
-            @pl.loop(0, slots)
+            @pl.loop(0, slots, unroll=4)
             def _(slot):
                 for parity in range(2):
                     value = jnp.concatenate(
@@ -359,13 +359,14 @@
             pl.semaphore_signal(barrier, inc=1, device_id=(belt, lon_away(away)), device_id_type=mesh_id)
 
         belt_peers(barrier)
+        waves_copy = pltpu.make_async_copy(waves_in_ref, waves_ref, small.at[0])
+        order_copy = pltpu.make_async_copy(order_in_ref, order_ref, small.at[1])
+        waves_copy.start()
+        order_copy.start()
 
         for chunk in range(CHUNKS):
             for item in range(chunk_items):
                 own_rows(chunk, item).start()
-        start_legendre(
-            jnp.broadcast_to(column_of(waves_ref[...], me, slots), (slots, LANES)), refs, mode_count, half
-        )
         pl.semaphore_wait(barrier, lons + belts - 2)
 
         @pl.loop(0, CHUNKS * chunk_items * 2)
@@ -378,6 +379,11 @@
                 gather(chunk, lons - away, item, lax.rem(index, 2)).start()
 
         belt_peers(ready)
+        waves_copy.wait()
+        order_copy.wait()
+        start_legendre(
+            jnp.broadcast_to(column_of(waves_ref[...], me, slots), (slots, LANES)), refs, mode_count, half
+        )
         fill_table(waves_ref, dft_ref, slots, owners, lon_count)
         legendre_range(0, EARLY)
         pl.semaphore_wait(ready, belts - 1)
@@ -430,12 +436,14 @@
         name="analyse",
         in_specs=[
             pl.BlockSpec(memory_space=pl.ANY),
-            pl.BlockSpec(memory_space=pltpu.VMEM),
-            pl.BlockSpec(memory_space=pltpu.SMEM),
+            pl.BlockSpec(memory_space=pltpu.HBM),
+            pl.BlockSpec(memory_space=pltpu.HBM),
         ],
         out_specs=pl.BlockSpec(memory_space=pltpu.VMEM),
         out_shape=jax.ShapeDtypeStruct((slots, rows, 2, half_modes), jnp.float32),
         scratch_shapes=[
+            pltpu.VMEM(waves.shape, jnp.int32),
+            pltpu.SMEM(field_order.shape, jnp.int32),
             pltpu.VMEM((owners * owner_rows, lon_count), jnp.bfloat16),
             pltpu.VMEM((slots, 2, half_modes, half), jnp.bfloat16),
             pltpu.VMEM((CHUNKS, lons, chunk_rows, lon_local), jnp.bfloat16),
@@ -455,12 +463,30 @@
             dma((CHUNKS,)),
             dma((CHUNKS, 2)),
             dma((CHUNKS,)),
+            dma((2,)),
             pltpu.SemaphoreType.REGULAR,
         ],
         compiler_params=pltpu.CompilerParams(
-            collective_id=0, has_side_effects=True, vmem_limit_bytes=60 << 20
+            collective_id=0, has_side_effects=True, vmem_limit_bytes=51 << 20
         ),
     )(grid_fields, waves, field_order)
+
+
+def hand_on(value):
+    def body(in_ref, out_ref, done):
+        copy = pltpu.make_async_copy(in_ref, out_ref, done)
+        copy.start()
+        copy.wait()
+
+    return pl.pallas_call(
+        body,
+        name="hand_on",
+        in_specs=[pl.BlockSpec(memory_space=pltpu.VMEM)],
+        out_specs=pl.BlockSpec(memory_space=pl.ANY),
+        out_shape=jax.ShapeDtypeStruct(value.shape, value.dtype),
+        scratch_shapes=[pltpu.SemaphoreType.DMA],
+        compiler_params=pltpu.CompilerParams(vmem_limit_bytes=4 << 20),
+    )(value)
 
 
 def on_device(grid_fields, field_order, wave_order):
@@ -469,8 +495,10 @@
     slots = mode_count // owners
     levels = grid_fields.shape[0]
     waves = wave_order.astype(jnp.int32).reshape(mode_count // LANES, LANES)
-    spectral = analyse(grid_fields, waves, field_order.astype(jnp.int32))
-    return spectral.reshape(slots, 2, levels, 2, mode_count // 2)
+    waves = pltpu.with_memory_space_constraint(waves, pltpu.HBM)
+    field_order = pltpu.with_memory_space_constraint(field_order.astype(jnp.int32), pltpu.HBM)
+    spectral = analyse(grid_fields, waves, field_order)
+    return hand_on(spectral).reshape(slots, 2, levels, 2, mode_count // 2)
 
 
 def solution(mesh):

time: 98.4 us -> 91.3 us (0.928)
  local copies, waits for them, and re-layouts: 3.81 us -> 0 us
  Pallas kernels: 94.4 us -> 91.2 us
    pallas_call x1, Pallas kernels: 94.4 us -> 89.9 us  [analyse(): pl.pallas_call(body, name='analyse', in_specs=[pl.BlockSpec(memory_space=...]
    unnamed x1 -> x0, local copies, waits for them, and re-layouts: 3.81 us -> none
    pallas_call x0 -> x1, Pallas kernels: none -> 1.33 us  [hand_on(): pl.pallas_call(body, name='hand_on', in_specs=[pl.BlockSpec(memory_space=...]
where the time goes in v2:
time: 91.3 us; the launch traced here: 91.2 us
  Pallas kernels  91.2 us (100%)
    pallas_call x1, Pallas kernels, analyse(): pl.pallas_call(body, name='analyse', in_specs=[pl.BlockSpec(memory_space=...  89.9 us

profile of v2, /device:TPU:1, one launch (start us, length us, event | category | flops | bytes accessed | tf_op | source)
XLA Modules:
  0.0 91.2 jit_solution(14643751801501104919)
XLA Ops:
  0.0 89.9 %analyse.1.in_ref = f32[8,64,2,512]{3,2,1,0:T(2,128)S(1)} custom-call(bf16[32,128,512]{2,1,0:T(8,128)(2,1)} %fields_ref.1, s32[8,128]{1,0:T(8,128)} %bitcast.2, s32[32]{0:T(128)} %order_in_ref.1), custom_call_target="tpu_custom_call" | custom-call | tf_op jit(solution)/shard_map/analyse/pallas_call | solution.py:434
  89.9 1.3 %hand_on.1 = f32[8,64,2,512]{3,2,1,0:T(2,128)} custom-call(f32[8,64,2,512]{3,2,1,0:T(2,128)S(1)} %analyse.1.in_ref), custom_call_target="tpu_custom_call" | custom-call | tf_op jit(solution)/shard_map/hand_on/pallas_call | solution.py:481

commit v3 on v2

--- a/solution.py
+++ b/solution.py
@@ -14,6 +14,7 @@
 CODE_LOW = -20.0
 
 CHUNKS = 2
+PIECES = 4
 BLOCK = 32
 RENORM = 16
 EARLY = 19
@@ -180,7 +181,7 @@
     rows = 2 * levels
     half_lons = lons // 2
     side_belts = belts // 4
-    piece = lat_local // 2
+    piece = lat_local // PIECES
     scale = 1.0 / math.sqrt(lon_count)
     mesh_id = pl.DeviceIdType.MESH
     legendre_steps = mode_count // BLOCK
@@ -229,19 +230,21 @@
                 in_local.at[chunk, item],
             )
 
-        def send(chunk, step, index):
-            core, target = member(index)
+        members = [member(index) for index in range(group)]
+
+        def send(chunk, step, block, index):
+            core, target = members[index]
             return pltpu.make_async_remote_copy(
                 send_ref.at[chunk, step, core * lons + target],
                 recv_ref.at[chunk, me],
                 out_send.at[chunk],
                 out_recv.at[chunk, side],
-                device_id=(place(step) * 2 + core, target),
+                device_id=(block * 2 + core, target),
                 device_id_type=mesh_id,
             )
 
         def own_block(chunk):
-            core, target = member(0)
+            core, target = members[0]
             return pltpu.make_async_copy(
                 send_ref.at[chunk, blocks - 1, core * lons + target], recv_ref.at[chunk, me], out_local.at[chunk]
             )
@@ -274,7 +277,8 @@
 
             @pl.loop(0, blocks)
             def _(step):
-                start = pl.multiple_of(place(step) * block_rows, block_rows)
+                block = place(step)
+                start = pl.multiple_of(block * block_rows, block_rows)
                 total = None
                 for part in range(lons):
                     term = lax.dot_general(
@@ -286,13 +290,12 @@
                     total = term if total is None else total + term
                 send_ref[chunk, step] = encode(total * scale).reshape(group, owner_rows, chunk_rows)
 
-                @pl.loop(0, group)
-                def _(back):
-                    index = group - 1 - back
-
-                    @pl.when((step < blocks - 1) | (index > 0))
-                    def _():
-                        send(chunk, step, index).start()
+                for index in range(group - 1, 0, -1):
+                    send(chunk, step, block, index).start()
+
+                @pl.when(step < blocks - 1)
+                def _():
+                    send(chunk, step, block, 0).start()
 
             own_block(chunk).start()
 
@@ -318,7 +321,7 @@
         def project(from_side, order, emit):
             start = pl.multiple_of(from_side * side_belts * lat_local, LANES)
 
-            @pl.loop(0, slots, unroll=4)
+            @pl.loop(0, slots, unroll=8)
             def _(slot):
                 for parity in range(2):
                     value = jnp.concatenate(
@@ -369,14 +372,14 @@
                 own_rows(chunk, item).start()
         pl.semaphore_wait(barrier, lons + belts - 2)
 
-        @pl.loop(0, CHUNKS * chunk_items * 2)
+        @pl.loop(0, CHUNKS * chunk_items * PIECES)
         def _(index):
-            chunk = index // (2 * chunk_items)
-            item = lax.rem(index // 2, chunk_items)
+            chunk = index // (PIECES * chunk_items)
+            item = lax.rem(index // PIECES, chunk_items)
 
             @pl.loop(1, lons)
             def _(away):
-                gather(chunk, lons - away, item, lax.rem(index, 2)).start()
+                gather(chunk, lons - away, item, lax.rem(index, PIECES)).start()
 
         belt_peers(ready)
         waves_copy.wait()

time: 91.3 us -> 90.6 us (level)
  no operation moved by 1% of the time
where the time goes in v3:
time: 90.6 us; the launch traced here: 90.5 us
  Pallas kernels  90.5 us (100%)
    pallas_call x1, Pallas kernels, analyse(): pl.pallas_call(body, name='analyse', in_specs=[pl.BlockSpec(memory_space=...  89.2 us

profile of v3, /device:TPU:1, one launch (start us, length us, event | category | flops | bytes accessed | tf_op | source)
XLA Modules:
  0.0 90.5 jit_solution(8443948579156962820)
XLA Ops:
  0.0 89.2 %analyse.1.in_ref = f32[8,64,2,512]{3,2,1,0:T(2,128)S(1)} custom-call(bf16[32,128,512]{2,1,0:T(8,128)(2,1)} %fields_ref.1, s32[8,128]{1,0:T(8,128)} %bitcast.2, s32[32]{0:T(128)} %order_in_ref.1), custom_call_target="tpu_custom_call" | custom-call | tf_op jit(solution)/shard_map/analyse/pallas_call | solution.py:437
  89.2 1.3 %hand_on.1 = f32[8,64,2,512]{3,2,1,0:T(2,128)} custom-call(f32[8,64,2,512]{3,2,1,0:T(2,128)S(1)} %analyse.1.in_ref), custom_call_target="tpu_custom_call" | custom-call | tf_op jit(solution)/shard_map/hand_on/pallas_call | solution.py:484

commit v4 on v3

--- a/solution.py
+++ b/solution.py
@@ -160,7 +160,7 @@
                 ].astype(jnp.bfloat16)
 
 
-def analyse(grid_fields, waves, field_order):
+def analyse(grid_fields, waves):
     belts = lax.axis_size("belt")
     lons = lax.axis_size("lon")
     levels, lat_local, lon_local = grid_fields.shape
@@ -181,13 +181,14 @@
     rows = 2 * levels
     half_lons = lons // 2
     side_belts = belts // 4
+    tiles = half_modes // LANES
     piece = lat_local // PIECES
     scale = 1.0 / math.sqrt(lon_count)
     mesh_id = pl.DeviceIdType.MESH
     legendre_steps = mode_count // BLOCK
 
     def body(
-        fields_ref, waves_in_ref, order_in_ref, out_ref, waves_ref, order_ref, dft_ref, leg_ref, rows_in_ref, send_ref, recv_ref, wide_ref, sum_ref,
+        fields_ref, waves_in_ref, out_ref, waves_ref, dft_ref, leg_ref, rows_in_ref, send_ref, recv_ref, wide_ref, sum_ref,
         prev_ref, cur_ref, scale_ref, inv_ref, geo_ref, step_rows_ref,
         in_send, in_recv, in_local, out_send, out_recv, out_local, small, ready,
     ):
@@ -318,7 +319,7 @@
                     wide_ref[0, near, chunk * chunk_items + item] = north + south
                     wide_ref[1, near, chunk * chunk_items + item] = north - south
 
-        def project(from_side, order, emit):
+        def project(from_side, emit):
             start = pl.multiple_of(from_side * side_belts * lat_local, LANES)
 
             @pl.loop(0, slots, unroll=8)
@@ -340,9 +341,7 @@
                         ],
                         axis=1,
                     )
-                    sums = jnp.dot(
-                        order, jnp.concatenate(split(value), axis=0), preferred_element_type=jnp.float32
-                    ).astype(jnp.bfloat16)
+                    sums = jnp.concatenate(split(value), axis=0)
                     result = lax.dot_general(
                         sums,
                         leg_ref[slot, parity, :, pl.ds(start, side_belts * lat_local)],
@@ -362,10 +361,8 @@
             pl.semaphore_signal(barrier, inc=1, device_id=(belt, lon_away(away)), device_id_type=mesh_id)
 
         belt_peers(barrier)
-        waves_copy = pltpu.make_async_copy(waves_in_ref, waves_ref, small.at[0])
-        order_copy = pltpu.make_async_copy(order_in_ref, order_ref, small.at[1])
+        waves_copy = pltpu.make_async_copy(waves_in_ref, waves_ref, small)
         waves_copy.start()
-        order_copy.start()
 
         for chunk in range(CHUNKS):
             for item in range(chunk_items):
@@ -383,7 +380,6 @@
 
         belt_peers(ready)
         waves_copy.wait()
-        order_copy.wait()
         start_legendre(
             jnp.broadcast_to(column_of(waves_ref[...], me, slots), (slots, LANES)), refs, mode_count, half
         )
@@ -394,20 +390,6 @@
         legendre_range(EARLY, legendre_steps)
         transform(1)
 
-        source = iota((2 * rows, 2 * rows), 0)
-        target = iota((2 * rows, 2 * rows), 1)
-        wanted = jnp.zeros((1, 2 * rows), jnp.int32)
-        for index in range(levels):
-            wanted = jnp.where(lax.rem(iota((1, 2 * rows), 1), levels) == index, order_ref[index], wanted)
-        within = lax.rem(source, rows)
-        level = lax.rem(within // 2, lons) * items + within // (2 * lons)
-        match = (
-            (level == wanted)
-            & (lax.rem(within, 2) == lax.rem(target, rows) // levels)
-            & (source // rows == target // rows)
-        )
-        order = jnp.where(match, 1.0, 0.0).T.astype(jnp.bfloat16)
-
         other_count = owners // 2
         for chunk in range(CHUNKS):
             exchanged(chunk, 1 - side, other_count).wait_recv()
@@ -421,13 +403,16 @@
             sum_ref[slot, parity] = value
 
         def finish(slot, parity, value):
-            out_ref[slot, :, parity, :] = sum_ref[slot, parity] + value
-
-        project(1 - side, order, keep)
+            value = sum_ref[slot, parity] + value
+            for tile in range(tiles):
+                start = slot * (rows * tiles * 2) + tile * 2 + parity
+                out_ref[pl.ds(start, rows, stride=2 * tiles), :] = value[:, tile * LANES : (tile + 1) * LANES]
+
+        project(1 - side, keep)
         own_block(CHUNKS - 1).wait()
         exchanged(CHUNKS - 1, side, other_count - 1).wait_recv()
         mirror_sums(CHUNKS - 1, side)
-        project(side, order, finish)
+        project(side, finish)
 
         for chunk in range(CHUNKS):
             gathered(chunk).wait_send()
@@ -440,13 +425,11 @@
         in_specs=[
             pl.BlockSpec(memory_space=pl.ANY),
             pl.BlockSpec(memory_space=pltpu.HBM),
-            pl.BlockSpec(memory_space=pltpu.HBM),
         ],
         out_specs=pl.BlockSpec(memory_space=pltpu.VMEM),
-        out_shape=jax.ShapeDtypeStruct((slots, rows, 2, half_modes), jnp.float32),
+        out_shape=jax.ShapeDtypeStruct((slots * rows * tiles * 2, LANES), jnp.float32),
         scratch_shapes=[
             pltpu.VMEM(waves.shape, jnp.int32),
-            pltpu.SMEM(field_order.shape, jnp.int32),
             pltpu.VMEM((owners * owner_rows, lon_count), jnp.bfloat16),
             pltpu.VMEM((slots, 2, half_modes, half), jnp.bfloat16),
             pltpu.VMEM((CHUNKS, lons, chunk_rows, lon_local), jnp.bfloat16),
@@ -466,30 +449,37 @@
             dma((CHUNKS,)),
             dma((CHUNKS, 2)),
             dma((CHUNKS,)),
-            dma((2,)),
+            dma,
             pltpu.SemaphoreType.REGULAR,
         ],
         compiler_params=pltpu.CompilerParams(
             collective_id=0, has_side_effects=True, vmem_limit_bytes=51 << 20
         ),
-    )(grid_fields, waves, field_order)
-
-
-def hand_on(value):
-    def body(in_ref, out_ref, done):
-        copy = pltpu.make_async_copy(in_ref, out_ref, done)
-        copy.start()
-        copy.wait()
+    )(grid_fields, waves)
+
+
+def hand_on(value, field_order, items, lons):
+    levels = items * lons
+
+    def body(order_ref, in_ref, out_ref, done):
+        for place in range(levels):
+            level = order_ref[place]
+            for component in range(2):
+                source = lax.rem(level, items) * (2 * lons) + lax.div(level, items) * 2 + component
+                pltpu.make_async_copy(
+                    in_ref.at[:, source], out_ref.at[:, component * levels + place], done
+                ).start()
+        pltpu.make_async_copy(in_ref, out_ref, done).wait()
 
     return pl.pallas_call(
         body,
         name="hand_on",
-        in_specs=[pl.BlockSpec(memory_space=pltpu.VMEM)],
+        in_specs=[pl.BlockSpec(memory_space=pltpu.SMEM), pl.BlockSpec(memory_space=pltpu.VMEM)],
         out_specs=pl.BlockSpec(memory_space=pl.ANY),
         out_shape=jax.ShapeDtypeStruct(value.shape, value.dtype),
         scratch_shapes=[pltpu.SemaphoreType.DMA],
         compiler_params=pltpu.CompilerParams(vmem_limit_bytes=4 << 20),
-    )(value)
+    )(field_order, value)
 
 
 def on_device(grid_fields, field_order, wave_order):
@@ -499,9 +489,11 @@
     levels = grid_fields.shape[0]
     waves = wave_order.astype(jnp.int32).reshape(mode_count // LANES, LANES)
     waves = pltpu.with_memory_space_constraint(waves, pltpu.HBM)
-    field_order = pltpu.with_memory_space_constraint(field_order.astype(jnp.int32), pltpu.HBM)
-    spectral = analyse(grid_fields, waves, field_order)
-    return hand_on(spectral).reshape(slots, 2, levels, 2, mode_count // 2)
+    spectral = analyse(grid_fields, waves).reshape(slots, 2 * levels, -1, LANES)
+    lons = lax.axis_size("lon")
+    spectral = hand_on(spectral, field_order.astype(jnp.int32), levels // lons, lons)
+    spectral = spectral.reshape(slots, 2, levels, -1, 2, LANES)
+    return jnp.swapaxes(spectral, 3, 4).reshape(slots, 2, levels, 2, mode_count // 2)
 
 
 def solution(mesh):

time: 90.6 us -> 88.6 us (0.978)
  Pallas kernels: 90.5 us -> 88.5 us
    pallas_call x1, Pallas kernels: 89.2 us -> 86.7 us  [analyse(): pl.pallas_call(body, name='analyse', in_specs=[pl.BlockSpec(memory_space=...]
where the time goes in v4:
time: 88.6 us; the launch traced here: 88.5 us
  Pallas kernels  88.5 us (100%)
    pallas_call x1, Pallas kernels, analyse(): pl.pallas_call(body, name='analyse', in_specs=[pl.BlockSpec(memory_space=...  86.7 us
    pallas_call x1, Pallas kernels, hand_on(): pl.pallas_call(body, name='hand_on', in_specs=[pl.BlockSpec(memory_space=...  1.84 us

profile of v4, /device:TPU:1, one launch (start us, length us, event | category | flops | bytes accessed | tf_op | source)
XLA Modules:
  0.0 88.5 jit_solution(17299200867693148839)
XLA Ops:
  0.0 0.0 copy-start
  0.0 86.7 %analyse.1 = f32[4096,128]{1,0:T(8,128)S(1)} custom-call(bf16[32,128,512]{2,1,0:T(8,128)(2,1)} %fields_ref.1, s32[8,128]{1,0:T(8,128)} %bitcast.8), custom_call_target="tpu_custom_call" | custom-call | tf_op jit(solution)/shard_map/analyse/pallas_call | solution.py:422
  86.7 0.0 copy-done
  86.7 1.8 %hand_on.1 = f32[8,64,8,128]{3,2,1,0:T(8,128)} custom-call(s32[32]{0:T(128)S(1)} %copy-done, f32[8,64,8,128]{3,2,1,0:T(8,128)S(1)} %bitcast.7), custom_call_target="tpu_custom_call" | custom-call | tf_op jit(solution)/shard_map/hand_on/pallas_call | solution.py:474
Async XLA Ops:
  0.0 86.7 %copy-start = (s32[32]{0:T(128)S(1)}, s32[32]{0:T(128)}, u32[]{:S(2)}) copy-start(s32[32]{0:T(128)} %order_ref.1) | copy-start | bytes 388

commit v5 on v4

--- a/solution.py
+++ b/solution.py
@@ -319,7 +319,7 @@
                     wide_ref[0, near, chunk * chunk_items + item] = north + south
                     wide_ref[1, near, chunk * chunk_items + item] = north - south
 
-        def project(from_side, emit):
+        def project(from_side, chosen, emit):
             start = pl.multiple_of(from_side * side_belts * lat_local, LANES)
 
             @pl.loop(0, slots, unroll=8)
@@ -333,7 +333,7 @@
                                         parity, from_side * side_belts + near, item,
                                         pl.ds(slot, 2 * lons, stride=slots), :,
                                     ]
-                                    for item in range(items)
+                                    for item in chosen
                                 ],
                                 axis=0,
                             )
@@ -348,7 +348,8 @@
                         NT_DIMS,
                         preferred_element_type=jnp.float32,
                     )
-                    emit(slot, parity, result[:rows] + result[rows:])
+                    half_rows = result.shape[0] // 2
+                    emit(slot, parity, result[:half_rows] + result[half_rows:])
 
         def belt_peers(semaphore):
             @pl.loop(1, belts)
@@ -391,6 +392,21 @@
         transform(1)
 
         other_count = owners // 2
+        early = rows - chunk_items * 2 * lons
+
+        def add(slot, parity, value):
+            sum_ref[slot, parity, :early] += value[:early]
+            sum_ref[slot, parity, early:] = value[early:]
+
+        def keep_early(slot, parity, value):
+            sum_ref[slot, parity, :early] = value
+
+        def finish(slot, parity, value):
+            value = jnp.concatenate((sum_ref[slot, parity, :early], sum_ref[slot, parity, early:] + value), axis=0)
+            for tile in range(tiles):
+                start = slot * (rows * tiles * 2) + tile * 2 + parity
+                out_ref[pl.ds(start, rows, stride=2 * tiles), :] = value[:, tile * LANES : (tile + 1) * LANES]
+
         for chunk in range(CHUNKS):
             exchanged(chunk, 1 - side, other_count).wait_recv()
             mirror_sums(chunk, 1 - side)
@@ -399,20 +415,14 @@
                 exchanged(chunk, side, other_count - 1).wait_recv()
                 mirror_sums(chunk, side)
 
-        def keep(slot, parity, value):
-            sum_ref[slot, parity] = value
-
-        def finish(slot, parity, value):
-            value = sum_ref[slot, parity] + value
-            for tile in range(tiles):
-                start = slot * (rows * tiles * 2) + tile * 2 + parity
-                out_ref[pl.ds(start, rows, stride=2 * tiles), :] = value[:, tile * LANES : (tile + 1) * LANES]
-
-        project(1 - side, keep)
+            if chunk == CHUNKS - 2:
+                project(side, range(items - chunk_items), keep_early)
+
+        project(1 - side, range(items), add)
         own_block(CHUNKS - 1).wait()
         exchanged(CHUNKS - 1, side, other_count - 1).wait_recv()
         mirror_sums(CHUNKS - 1, side)
-        project(side, finish)
+        project(side, range(items - chunk_items, items), finish)
 
         for chunk in range(CHUNKS):
             gathered(chunk).wait_send()

time: 88.6 us -> 88.4 us (level)
  no operation moved by 1% of the time
where the time goes in v5:
time: 88.4 us; the launch traced here: 88.3 us
  Pallas kernels  88.3 us (100%)
    pallas_call x1, Pallas kernels, analyse(): pl.pallas_call(body, name='analyse', in_specs=[pl.BlockSpec(memory_space=...  86.5 us
    pallas_call x1, Pallas kernels, hand_on(): pl.pallas_call(body, name='hand_on', in_specs=[pl.BlockSpec(memory_space=...  1.84 us

profile of v5, /device:TPU:1, one launch (start us, length us, event | category | flops | bytes accessed | tf_op | source)
XLA Modules:
  0.0 88.3 jit_solution(11079873212233901355)
XLA Ops:
  0.0 0.0 copy-start
  0.0 86.5 %analyse.1 = f32[4096,128]{1,0:T(8,128)S(1)} custom-call(bf16[32,128,512]{2,1,0:T(8,128)(2,1)} %fields_ref.1, s32[8,128]{1,0:T(8,128)} %bitcast.8), custom_call_target="tpu_custom_call" | custom-call | tf_op jit(solution)/shard_map/analyse/pallas_call | solution.py:432
  86.5 0.0 copy-done
  86.5 1.8 %hand_on.1 = f32[8,64,8,128]{3,2,1,0:T(8,128)} custom-call(s32[32]{0:T(128)S(1)} %copy-done, f32[8,64,8,128]{3,2,1,0:T(8,128)S(1)} %bitcast.7), custom_call_target="tpu_custom_call" | custom-call | tf_op jit(solution)/shard_map/hand_on/pallas_call | solution.py:484
Async XLA Ops:
  0.0 86.5 %copy-start = (s32[32]{0:T(128)S(1)}, s32[32]{0:T(128)}, u32[]{:S(2)}) copy-start(s32[32]{0:T(128)} %order_ref.1) | copy-start | bytes 388
